TPU v7x, 256 devices: a whole 4x4x8 slice. The times are simulated.
256 devices in a mesh: seq: 64 (over x, z, core), head: 4 (over y).
Axes of the slice: x: 4, y: 4, z: 8, core: 2. Of those that a mesh axis runs over, the one named last changes fastest.
Arguments:
- tokens: bfloat16 [65536, 2048], P('seq', 'head'), may hold values from -6 to 6
- w_qkv: bfloat16 [2048, 6144], P(None, 'head'), may hold values from -1 to 1
- item_at: int32 [4, 2048], P('head'), may hold values from 0 to 2047, as said below
- rand_cols: int32 [16, 512, 4], P('head'), may hold values from 0 to 511, as said below
- rand_used: int32 [16, 512], P('head'), may hold values from 0 to 4, as said below
Outputs:
- attended: bfloat16 [4, 2048, 128, 128], P('head', 'seq')
Inputs may be any that keep to these rules, and one draw needn't show every extreme that they name: In head group g, item e * 512 + r stands for head g * 4 + e at block row r, and every item appears exactly once in item_at[g]. Positions j * 32 to (j + 1) * 32 - 1 hold the items placed at device j of seq. Of the items whose block rows lie on one device of seq, at most 1 of one group are placed at any one device, and exactly 1 at some. `rand_cols`: take all 128 candidates (used or not) of the items placed at one device in one head group, or of the items of one group whose block rows lie on one device: at most 2 of them lie in the block rows of any one device of seq, and exactly 2 in some. A candidate may equal a window block or block 0. `rand_used`: in each head group the counts of the 32 items placed at one device sum to exactly 64; the sums over the items whose block rows lie on one device vary.
All inputs are finite; a program needn't handle non-finite values.
Results may differ from a plain program's by a relative error of at most 0.019.
Values may be sent and summed in bfloat16 or wider, within the bound.
No kernel may reach another device: no remote copies, remote signals or barrier semaphores. Data moves between devices by JAX's collectives and lax.ppermute only.
A program may use at most 128 MiB of HBM per device.

v0:
```python
import math
import jax
import jax.numpy as jnp
from jax import lax
from jax.sharding import PartitionSpec as P

neg_large = -1e30


def extended(block, sides, width):
    for axis, dim in sides:
        count = lax.axis_size(axis)
        forward = [(i, i + 1) for i in range(count - 1)]
        backward = [(target, source) for source, target in forward]
        low = lax.ppermute(
            lax.slice_in_dim(block, block.shape[dim] - width, None, axis=dim), axis, forward
        )
        high = lax.ppermute(lax.slice_in_dim(block, 0, width, axis=dim), axis, backward)
        block = jnp.concatenate([low, block, high], axis=dim)
    return block


def broadcast(block, axis, owner):
    block = jnp.where(lax.axis_index(axis) == owner, block, jnp.zeros_like(block))
    return lax.psum(block, axis)


def packed_attend(
    queries, near_keys, near_values, near_usable, rand_keys, rand_values, slot_item, factor
):
    item_count = queries.shape[0]
    near_scores = (
        jnp.einsum("ibe,ijke->ibjk", queries, near_keys, preferred_element_type=jnp.float32)
        * factor
    )
    near_scores = jnp.where(near_usable[:, None, :, None], near_scores, neg_large)
    rand_scores = (
        jnp.einsum(
            "kbe,kce->kbc", queries[slot_item], rand_keys, preferred_element_type=jnp.float32
        )
        * factor
    )
    member = slot_item[None, :] == jnp.arange(item_count, dtype=jnp.int32)[:, None]
    slot_max = jnp.max(rand_scores, axis=2)
    rand_max = jnp.max(jnp.where(member[:, :, None], slot_max[None], neg_large), axis=1)
    row_max = jnp.maximum(jnp.max(near_scores, axis=(2, 3)), rand_max)
    near_expo = jnp.exp(near_scores - row_max[:, :, None, None])
    rand_expo = jnp.exp(rand_scores - row_max[slot_item][:, :, None])
    slot_total = jnp.sum(rand_expo, axis=2)
    row_sum = jnp.sum(near_expo, axis=(2, 3)) + jnp.sum(
        jnp.where(member[:, :, None], slot_total[None], 0.0), axis=1
    )
    summed = jnp.einsum(
        "ibjk,ijke->ibe",
        near_expo.astype(jnp.bfloat16),
        near_values,
        preferred_element_type=jnp.float32,
    )
    slot_out = jnp.einsum(
        "kbc,kce->kbe",
        rand_expo.astype(jnp.bfloat16),
        rand_values,
        preferred_element_type=jnp.float32,
    )
    summed = summed + jnp.einsum(
        "ik,kbe->ibe", member.astype(jnp.float32), slot_out, precision=lax.Precision.HIGHEST
    )
    return (summed, row_max, row_sum)


def rank_among(homes):
    count = homes.shape[-1]
    earlier = jnp.tril(jnp.ones((count, count), bool), -1)
    same_home = homes[..., :, None] == homes[..., None, :]
    return jnp.sum(same_home & earlier, axis=-1)


def pack_live(counts, rand_count, live_total):
    slot_total = counts.shape[0] * rand_count
    slot_ids = jnp.arange(slot_total, dtype=jnp.int32)
    live = slot_ids % rand_count < jnp.repeat(counts, rand_count)
    live_rank = jnp.cumsum(live.astype(jnp.int32)) - 1
    picks = live[:, None] & (live_rank[:, None] == jnp.arange(live_total, dtype=jnp.int32)[None, :])
    return jnp.sum(jnp.where(picks, slot_ids[:, None], 0), axis=0)


def local(tokens, w_qkv, item_at, rand_cols, rand_used):
    seq_count = lax.axis_size("seq")
    my_seq = lax.axis_index("seq")
    heads_dev, nblocks, rand_count = rand_cols.shape
    tokens_dev = tokens.shape[0]
    head_dim = w_qkv.shape[1] // (3 * heads_dev)
    block_len = tokens_dev * seq_count // nblocks
    rows_dev = tokens_dev // block_len
    items_dev = heads_dev * rows_dev
    slot_count = items_dev * rand_count
    live_total = slot_count // 2
    cap_items = max(1, items_dev // seq_count)
    cap_tiles = max(1, slot_count // seq_count)
    factor = 1.0 / math.sqrt(head_dim)
    projected = jnp.dot(
        lax.all_gather(tokens, "head", axis=1, tiled=True),
        w_qkv,
        preferred_element_type=jnp.float32,
    )
    projected = projected.astype(jnp.bfloat16).reshape(rows_dev, block_len, 3, heads_dev, head_dim)
    query_tiles = projected[:, :, 0].transpose(2, 0, 1, 3).reshape(items_dev, block_len, head_dim)
    pair_rows = projected[:, :, 1:].reshape(tokens_dev, 2, heads_dev, head_dim)
    widened = extended(pair_rows, (("seq", 0),), block_len)
    pair_tiles = widened.reshape(rows_dev + 2, block_len, 2, heads_dev, head_dim).transpose(
        3, 0, 2, 1, 4
    )
    own_tiles = pair_tiles[:, 1 : rows_dev + 1].reshape(items_dev, 2, block_len, head_dim)
    first_tiles = broadcast(pair_tiles[:, 1], "seq", 0)
    window_tiles = jnp.stack(
        [
            pair_tiles[:, 0:rows_dev],
            pair_tiles[:, 1 : rows_dev + 1],
            pair_tiles[:, 2 : rows_dev + 2],
        ],
        axis=2,
    )
    window_tiles = window_tiles.reshape(items_dev, 3, 2, block_len, head_dim)
    placed = item_at[0].reshape(seq_count, items_dev)
    placed_head = placed // nblocks
    placed_row = placed % nblocks
    placed_home = placed_row // rows_dev
    local_index = placed_head * rows_dev + placed_row % rows_dev
    is_mine = placed_home == my_seq
    rank_mine = jnp.cumsum(is_mine.astype(jnp.int32), axis=1) - 1
    slot_ids = jnp.arange(cap_items, dtype=jnp.int32)
    slot_hit = is_mine[:, :, None] & (rank_mine[:, :, None] == slot_ids)
    send_index = jnp.sum(jnp.where(slot_hit, local_index[:, :, None], 0), axis=1).reshape(-1)
    my_items = lax.dynamic_index_in_dim(placed, my_seq, 0, keepdims=False)
    item_head = my_items // nblocks
    item_row = my_items % nblocks
    item_home = item_row // rows_dev
    recv_slot = item_home * cap_items + rank_among(item_home)
    my_random = rand_cols[item_head, item_row].reshape(-1)
    tile_home = my_random // rows_dev
    tile_rank = rank_among(tile_home)
    tile_slot = tile_home * cap_tiles + tile_rank
    tile_ids = jnp.arange(cap_tiles, dtype=jnp.int32)
    peer_ids = jnp.arange(seq_count, dtype=jnp.int32)
    slot_head = jnp.repeat(item_head, rand_count)
    tile_local = slot_head * rows_dev + my_random % rows_dev
    wanted = (tile_home[None, :, None] == peer_ids[:, None, None]) & (
        tile_rank[None, :, None] == tile_ids[None, None, :]
    )
    requests = jnp.sum(jnp.where(wanted, tile_local[None, :, None], 0), axis=1)
    asked = lax.all_to_all(requests, "seq", split_axis=0, concat_axis=0, tiled=True)
    picked = own_tiles[asked.reshape(-1)].reshape(asked.shape + own_tiles.shape[1:])
    fetched = lax.all_to_all(picked, "seq", split_axis=0, concat_axis=0, tiled=True)
    gathered = fetched.reshape(seq_count * cap_tiles, 2, block_len, head_dim)[tile_slot]
    random_tiles = gathered.reshape(items_dev, rand_count, 2, block_len, head_dim)
    item_counts = rand_used[item_head, item_row]
    live_slots = pack_live(item_counts, rand_count, live_total)
    packed_tiles = random_tiles.reshape(slot_count, 2, block_len, head_dim)[live_slots]
    slot_item = live_slots // rand_count
    global_tiles = first_tiles[item_head][:, None]
    sent_query = query_tiles[send_index].reshape(seq_count, cap_items, block_len, head_dim)
    sent_window = window_tiles[send_index].reshape(seq_count, cap_items, 3, 2, block_len, head_dim)
    got_query, got_window = (
        lax.all_to_all(sent_query, "seq", split_axis=0, concat_axis=0, tiled=True),
        lax.all_to_all(sent_window, "seq", split_axis=0, concat_axis=0, tiled=True),
    )
    queries = got_query.reshape(seq_count * cap_items, block_len, head_dim)[recv_slot]
    windows = got_window.reshape(seq_count * cap_items, 3, 2, block_len, head_dim)[recv_slot]
    near_tiles = jnp.concatenate([windows, global_tiles], axis=1)
    near_usable = jnp.concatenate(
        [
            (item_row >= 1)[:, None],
            jnp.ones((items_dev, 1), bool),
            (item_row + 1 < nblocks)[:, None],
            jnp.ones((items_dev, 1), bool),
        ],
        axis=1,
    )
    summed, row_max, row_sum = packed_attend(
        queries,
        near_tiles[:, :, 0],
        near_tiles[:, :, 1],
        near_usable,
        packed_tiles[:, 0],
        packed_tiles[:, 1],
        slot_item,
        factor,
    )
    result = (summed / row_sum[:, :, None]).astype(jnp.bfloat16)
    return result.reshape(1, items_dev, block_len, head_dim)


def solution(mesh):
    return jax.shard_map(
        local,
        mesh=mesh,
        in_specs=(
            P("seq", "head"),
            P(None, "head"),
            P("head", None),
            P("head", None, None),
            P("head", None),
        ),
        out_specs=P("head", "seq", None, None),
        check_vma=False,
    )
```

profile of v0, /device:TPU:1, one launch (start us, length us, event | category | flops | bytes accessed | tf_op | source)
XLA Modules:
  0.0 679.1 jit_solution(8968216010016144075)
XLA Ops:
  13.3 13.0 %all-to-all-start.2 = ((s32[64,1,2]{2,1,0:T(1,128)}), s32[64,1,2]{2,1,0:T(1,128)S(1)}, u32[]{:S(2)}, u32[]{:S(2)}) async-start(s32[64,1,2]{2,1,0:T(1,128)} %copy.118), calls=%async_computation.2 | async-start | bytes 65536 | tf_op jit(solution)/shard_map/all_to_all | solution.py:151
  27.5 36.4 %all-gather.2.cloned.1.call-done = bf16[1024,2048]{1,0:T(8,128)(2,1)} async-done(((bf16[1024,512]{1,0:T(8,128)(2,1)}), bf16[1024,2048]{1,0:T(8,128)(2,1)}) %all-gather.2.cloned.1.call-update) | async-done | bytes 4194320 | tf_op jit(solution)/shard_map/all_gather | solution.py:102
  63.8 11.2 %convolution_convert_fusion = bf16[1024,1536]{1,0:T(8,128)(2,1)} fusion(bf16[1024,2048]{1,0:T(8,128)(2,1)} %all-gather.2.cloned.1.call-done, bf16[2048,1536]{1,0:T(8,128)(2,1)} %param.6), kind=kOutput, calls=%fused_computation.35 | convolution fusion | flops 6444023808 | bytes 13631488 | tf_op jit(solution)/shard_map/dot_general | solution.py:101
  75.0 5.0 reshape.931
  81.6 3.3 gather_fusion
  85.0 10.9 %all-to-all-start = ((bf16[64,1,128,128]{3,2,1,0:T(8,128)(2,1)}), bf16[64,1,128,128]{3,2,1,0:T(8,128)(2,1)}, u32[]{:S(2)}, u32[]{:S(2)}) async-start(bf16[64,1,128,128]{3,2,1,0:T(8,128)(2,1)} %bitcast.166), calls=%async_computation | async-start | bytes 4194304 | tf_op jit(solution)/shard_map/all_to_all | solution.py:164
  96.8 3.5 collective-permute-start
  101.1 2.1 collective-permute-start.1
  105.3 38.3 %collective-permute-done = bf16[128,2,4,128]{3,0,2,1:T(8,128)(2,1)S(1)} collective-permute-done((bf16[128,2,4,128]{3,0,2,1:T(8,128)(2,1)}, bf16[128,2,4,128]{3,0,2,1:T(8,128)(2,1)S(1)}, u32[]{:S(2)}, u32[]{:S(2)}) %collective-permute-start) | collective-permute-done | bytes 262176 | tf_op jit(solution)/shard_map/ppermute | solution.py:15
  143.6 2.4 collective-permute-done.1
  147.5 3.7 fusion.86
  151.4 6.7 gather_fusion.8
  158.0 9.3 %all-to-all-start.3 = ((bf16[64,2,2,128,128]{4,3,2,1,0:T(8,128)(2,1)}), bf16[64,2,2,128,128]{4,3,2,1,0:T(8,128)(2,1)}, u32[]{:S(2)}, u32[]{:S(2)}) async-start(bf16[64,2,2,128,128]{4,3,2,1,0:T(8,128)(2,1)} %bitcast.161), calls=%async_computation.3 | async-start | bytes 16777216 | tf_op jit(solution)/shard_map/all_to_all | solution.py:153
  167.4 1.9 copy.109
  169.8 3.3 pad_maximum_fusion
  173.1 10.0 %gather_fusion.2 = bf16[64,3,2,128,128]{4,3,2,1,0:T(8,128)(2,1)} fusion(bf16[32,3,2,128,128]{4,3,2,0,1:T(8,128)(2,1)} %pad_maximum_fusion, s32[1024]{0:T(1024)S(1)} %pad_clamp_fusion.6), kind=kCustom, calls=%fused_computation.2 | custom fusion | bytes 25166080 | tf_op jit(solution)/shard_map/gather | solution.py:162
  183.1 170.1 %all-to-all-done.3 = bf16[64,2,2,128,128]{4,3,2,1,0:T(8,128)(2,1)} async-done(((bf16[64,2,2,128,128]{4,3,2,1,0:T(8,128)(2,1)}), bf16[64,2,2,128,128]{4,3,2,1,0:T(8,128)(2,1)}, u32[]{:S(2)}, u32[]{:S(2)}) %all-to-all-start.3) | async-done | bytes 8388640 | tf_op jit(solution)/shard_map/all_to_all | solution.py:153
  353.1 6.2 all-to-all-start.1
  363.3 221.0 %all-reduce.2.cloned.1.call-done = bf16[4,2,128,128]{3,2,1,0:T(8,128)(2,1)} async-done(((bf16[4,2,128,128]{3,2,1,0:T(8,128)(2,1)}), bf16[4,2,128,128]{3,2,1,0:T(8,128)(2,1)}) %all-reduce.2.cloned.1.call-update) | async-done | bytes 262160 | tf_op jit(solution)/shard_map/psum | solution.py:25
  584.3 1.9 gather_fusion.4
  587.7 2.3 gather_fusion.1
  591.0 10.0 %gather_fusion.9 = bf16[128,2,128,128]{3,2,1,0:T(8,128)(2,1)} fusion(bf16[128,2,128,128]{3,2,1,0:T(8,128)(2,1)} %bitcast.37, s32[1024]{0:T(1024)S(1)} %pad_clamp_fusion.1), kind=kCustom, calls=%fused_computation.9 | custom fusion | bytes 16777728 | tf_op jit(solution)/shard_map/gather | solution.py:154
  601.0 6.4 gather_fusion.10
  607.4 5.2 multiply_reduce_fusion
  613.1 25.2 %all-to-all-done.1 = bf16[64,1,3,2,128,128]{5,4,3,2,1,0:T(8,128)(2,1)} async-done(((bf16[64,1,3,2,128,128]{5,4,3,2,1,0:T(8,128)(2,1)}), bf16[64,1,3,2,128,128]{5,4,3,2,1,0:T(8,128)(2,1)}, u32[]{:S(2)}, u32[]{:S(2)}) %all-to-all-start.1) | async-done | bytes 12582944 | tf_op jit(solution)/shard_map/all_to_all | solution.py:165
  638.3 8.7 %gather_fusion.3 = bf16[32,3,2,128,128]{4,3,2,1,0:T(8,128)(2,1)} fusion(bf16[64,3,2,128,128]{4,3,2,1,0:T(8,128)(2,1)} %bitcast.26, s32[1024]{0:T(1024)S(1)} %pad_clamp_fusion.5), kind=kCustom, calls=%fused_computation.3 | custom fusion | bytes 12583040 | tf_op jit(solution)/shard_map/gather | solution.py:168
  647.0 5.5 fusion
  653.1 3.3 fusion.18
  656.6 2.7 fusion.20
  660.6 2.1 fusion.1
  662.7 4.1 fusion.12
  666.8 5.5 fusion.31
  (100 shorter events, 24.1 us)
Async XLA Ops:
  6.5 353.1 %copy-start = (s32[4,512]{1,0:T(4,128)S(1)}, s32[4,512]{1,0:T(4,128)}, u32[]{:S(2)}) copy-start(s32[4,512]{1,0:T(4,128)} %param.9) | copy-start | bytes 24580
  6.5 57.3 %all-gather.2.cloned.1.call-start = ((), (), s32[]{:S(2)}) async-start(), calls=%async_computation.4 | async-start | bytes 5242880 | tf_op jit(solution)/shard_map/all_gather | solution.py:102
  13.3 71.7 %all-to-all-start.2 = ((s32[64,1,2]{2,1,0:T(1,128)}), s32[64,1,2]{2,1,0:T(1,128)S(1)}, u32[]{:S(2)}, u32[]{:S(2)}) async-start(s32[64,1,2]{2,1,0:T(1,128)} %copy.118), calls=%async_computation.2 | async-start | bytes 65536 | tf_op jit(solution)/shard_map/all_to_all | solution.py:151
  85.0 73.1 %all-to-all-start = ((bf16[64,1,128,128]{3,2,1,0:T(8,128)(2,1)}), bf16[64,1,128,128]{3,2,1,0:T(8,128)(2,1)}, u32[]{:S(2)}, u32[]{:S(2)}) async-start(bf16[64,1,128,128]{3,2,1,0:T(8,128)(2,1)} %bitcast.166), calls=%async_computation | async-start | bytes 4194304 | tf_op jit(solution)/shard_map/all_to_all | solution.py:164
  96.8 46.8 %collective-permute-start = (bf16[128,2,4,128]{3,0,2,1:T(8,128)(2,1)}, bf16[128,2,4,128]{3,0,2,1:T(8,128)(2,1)S(1)}, u32[]{:S(2)}, u32[]{:S(2)}) collective-permute-start(bf16[128,2,4,128]{3,0,2,1:T(8,128)(2,1)} %bitcast.157), channel_id=1, source_target_pairs={{0,4},{4,8},{8,12},{12,16},{16,20},{20,24},{24,28},{28,32},{32,36}... | collective-permute-start | bytes 786440 | tf_op jit(solution)/shard_map/ppermute | solution.py:15
  101.1 44.9 %collective-permute-start.1 = (bf16[128,2,4,128]{3,0,2,1:T(8,128)(2,1)}, bf16[128,2,4,128]{3,0,2,1:T(8,128)(2,1)}, u32[]{:S(2)}, u32[]{:S(2)}) collective-permute-start(bf16[128,2,4,128]{3,0,2,1:T(8,128)(2,1)} %bitcast.156), channel_id=1, source_target_pairs={{4,0},{8,4},{12,8},{16,12},{20,16},{24,20},{28,24},{32,28},{36,32}... | collective-permute-start | bytes 786440 | tf_op jit(solution)/shard_map/ppermute | solution.py:18
  147.5 3.8 copy-start.3
  158.0 195.1 %all-to-all-start.3 = ((bf16[64,2,2,128,128]{4,3,2,1,0:T(8,128)(2,1)}), bf16[64,2,2,128,128]{4,3,2,1,0:T(8,128)(2,1)}, u32[]{:S(2)}, u32[]{:S(2)}) async-start(bf16[64,2,2,128,128]{4,3,2,1,0:T(8,128)(2,1)} %bitcast.161), calls=%async_computation.3 | async-start | bytes 16777216 | tf_op jit(solution)/shard_map/all_to_all | solution.py:153
  167.3 2.2 copy-start.5
  353.1 7.9 %copy-start.7 = (s32[32]{0:T(128)S(1)}, s32[32]{0:T(128)}, u32[]{:S(2)}) copy-start(s32[32]{0:T(128)} %get-tuple-element.21) | copy-start | bytes 388
  353.1 285.1 %all-to-all-start.1 = ((bf16[64,1,3,2,128,128]{5,4,3,2,1,0:T(8,128)(2,1)}), bf16[64,1,3,2,128,128]{5,4,3,2,1,0:T(8,128)(2,1)}, u32[]{:S(2)}, u32[]{:S(2)}) async-start(bf16[64,1,3,2,128,128]{5,4,3,2,1,0:T(8,128)(2,1)} %bitcast.160), calls=%async_computation.1 | async-start | bytes 25165824 | tf_op jit(solution)/shard_map/all_to_all | solution.py:165
  359.3 225.0 %all-reduce.2.cloned.1.call-start = ((), (), s32[]{:S(2)}) async-start(), calls=%async_computation.5 | async-start | bytes 524288 | tf_op jit(solution)/shard_map/psum | solution.py:25
  638.3 8.7 %copy-start.6 = (bf16[32,2,128,128]{3,2,0,1:T(8,128)(2,1)S(1)}, bf16[32,2,128,128]{3,2,0,1:T(8,128)(2,1)}, u32[]{:S(2)}) copy-start(bf16[32,2,128,128]{3,2,0,1:T(8,128)(2,1)} %copy.158) | copy-start | bytes 6291460
  653.1 3.4 copy-start.2
  656.6 4.0 copy-start.4
  656.6 10.2 %slice-start = ((s8[6291456]{0:T(1024)(128)(4,1)}), s8[4194304]{0:T(1024)(128)(4,1)S(1)}, s32[]{:S(2)}) async-start(s8[6291456]{0:T(1024)(128)(4,1)} %bitcast.170), calls=%async_computation.6 | async-start | bytes 8388608
  660.6 6.2 slice-start.1
  666.8 5.5 copy-start.1
Sparse Core Ops, SparseCore 0:
  9.2 54.5 all-gather.1
  363.6 220.6 all-reduce.1
where the time goes:
time: 680 us; the launch traced here: 679 us
  waiting for transfers between devices  494 us (73%)
  local copies, waits for them, and re-layouts  75.2 us (11%)
  starting transfers between devices  45.3 us (7%)
  matrix products  34.2 us (5%)
  other arithmetic  16.5 us (2%)
  between operations  13.8 us (2%)
    psum x1, waiting for transfers between devices, broadcast(): return lax.psum(block, axis)  221 us
    all_to_all x1, waiting for transfers between devices, local(): lax.all_to_all(picked, 'seq', split_axis=0, concat_axis=0, tiled=True)  170 us
    ppermute x1, waiting for transfers between devices, extended(): lax.ppermute(lax.slice_in_dim(block, block.shape[dim] - width, None, axis...  38.3 us
    all_gather x1, waiting for transfers between devices, local(): lax.all_gather(tokens, 'head', axis=1, tiled=True)  36.4 us
    all_to_all x1, waiting for transfers between devices, local(): lax.all_to_all(sent_window, 'seq', split_axis=0, concat_axis=0, tiled=True)  25.2 us
  transfers between devices with their start and end apart: 8, of which 6 were waited for; matrix products, arithmetic and copies ran while one was open for 14% of the time, Pallas kernels for 0%

commit v1 on v0

--- a/solution.py
+++ b/solution.py
@@ -99,7 +99,9 @@
     cap_tiles = max(1, slot_count // seq_count)
     factor = 1.0 / math.sqrt(head_dim)
     projected = jnp.dot(
-        lax.all_gather(tokens, "head", axis=1, tiled=True),
+        jnp.concatenate(
+            lax.all_to_all(jnp.stack([tokens] * lax.axis_size("head")), "head", 0, 0), axis=1
+        ),
         w_qkv,
         preferred_element_type=jnp.float32,
     )

time: 680 us -> 694 us (1.021)
    all_to_all x0 -> x1, waiting for transfers between devices: none -> 42 us  [local(): lax.all_to_all(jnp.stack([tokens] * lax.axis_size('head')), 'head', 0, 0)]
    all_gather x1 -> x0, waiting for transfers between devices: 36.4 us -> none  [local(): lax.all_gather(tokens, 'head', axis=1, tiled=True)]
  transfers between devices with their start and end apart: 8 -> 8, of which waited for: 6 -> 6; matrix products, arithmetic and copies ran while one was open for 14% -> 13% of each run, Pallas kernels for 0% -> 0%
where the time goes in v1:
time: 694 us; the launch traced here: 693 us
  waiting for transfers between devices  499 us (72%)
  local copies, waits for them, and re-layouts  77.8 us (11%)
  starting transfers between devices  51.9 us (7%)
  matrix products  34.5 us (5%)
  other arithmetic  15.8 us (2%)
  between operations  13.8 us (2%)
    psum x1, waiting for transfers between devices, broadcast(): return lax.psum(block, axis)  222 us
    all_to_all x1, waiting for transfers between devices, local(): lax.all_to_all(picked, 'seq', split_axis=0, concat_axis=0, tiled=True)  170 us
    all_to_all x1, waiting for transfers between devices, local(): lax.all_to_all(jnp.stack([tokens] * lax.axis_size('head')), 'head', 0, 0)  42 us
    ppermute x1, waiting for transfers between devices, extended(): lax.ppermute(lax.slice_in_dim(block, block.shape[dim] - width, None, axis...  38.3 us
    all_to_all x1, waiting for transfers between devices, local(): lax.all_to_all(sent_window, 'seq', split_axis=0, concat_axis=0, tiled=True)  24.5 us
    all_to_all x1, starting transfers between devices, local(): lax.all_to_all(requests, 'seq', split_axis=0, concat_axis=0, tiled=True)  14.9 us
  transfers between devices with their start and end apart: 8, of which 6 were waited for; matrix products, arithmetic and copies ran while one was open for 13% of the time, Pallas kernels for 0%

profile of v1, /device:TPU:1, one launch (start us, length us, event | category | flops | bytes accessed | tf_op | source)
XLA Modules:
  0.0 692.9 jit_solution(15917607779844787802)
XLA Ops:
  8.0 2.5 stack.19
  10.6 5.1 all-to-all-start
  20.8 42.0 %all-to-all-done = bf16[4,1024,512]{1,2,0:T(8,128)(2,1)} async-done(((bf16[4,1024,512]{1,2,0:T(8,128)(2,1)}), bf16[4,1024,512]{1,2,0:T(8,128)(2,1)}, u32[]{:S(2)}, u32[]{:S(2)}) %all-to-all-start) | async-done | bytes 4194336 | tf_op jit(solution)/shard_map/all_to_all | solution.py:103
  62.8 14.9 %all-to-all-start.3 = ((s32[64,1,2]{2,1,0:T(1,128)}), s32[64,1,2]{2,1,0:T(1,128)S(1)}, u32[]{:S(2)}, u32[]{:S(2)}) async-start(s32[64,1,2]{2,1,0:T(1,128)} %copy.122), calls=%async_computation.3 | async-start | bytes 65536 | tf_op jit(solution)/shard_map/all_to_all | solution.py:153
  77.7 11.5 %convolution_convert_fusion = bf16[1024,1536]{1,0:T(8,128)(2,1)} fusion(bf16[1024,2048]{0,1:T(8,128)(2,1)} %bitcast.2, bf16[2048,1536]{1,0:T(8,128)(2,1)} %param.6), kind=kOutput, calls=%fused_computation.35 | convolution fusion | flops 6444023808 | bytes 13631488 | tf_op jit(solution)/shard_map/dot_general | solution.py:101
  89.2 5.0 reshape.941
  95.8 3.3 gather_fusion
  99.1 10.5 %all-to-all-start.1 = ((bf16[64,1,128,128]{3,2,1,0:T(8,128)(2,1)}), bf16[64,1,128,128]{3,2,1,0:T(8,128)(2,1)}, u32[]{:S(2)}, u32[]{:S(2)}) async-start(bf16[64,1,128,128]{3,2,1,0:T(8,128)(2,1)} %bitcast.169), calls=%async_computation.1 | async-start | bytes 4194304 | tf_op jit(solution)/shard_map/all_to_all | solution.py:166
  110.6 3.5 collective-permute-start
  114.8 2.1 collective-permute-start.1
  119.1 38.3 %collective-permute-done = bf16[128,2,4,128]{3,0,2,1:T(8,128)(2,1)S(1)} collective-permute-done((bf16[128,2,4,128]{3,0,2,1:T(8,128)(2,1)}, bf16[128,2,4,128]{3,0,2,1:T(8,128)(2,1)S(1)}, u32[]{:S(2)}, u32[]{:S(2)}) %collective-permute-start) | collective-permute-done | bytes 262176 | tf_op jit(solution)/shard_map/ppermute | solution.py:15
  157.3 2.4 collective-permute-done.1
  161.2 3.7 fusion.86
  165.1 6.7 gather_fusion.8
  171.8 9.3 %all-to-all-start.4 = ((bf16[64,2,2,128,128]{4,3,2,1,0:T(8,128)(2,1)}), bf16[64,2,2,128,128]{4,3,2,1,0:T(8,128)(2,1)}, u32[]{:S(2)}, u32[]{:S(2)}) async-start(bf16[64,2,2,128,128]{4,3,2,1,0:T(8,128)(2,1)} %bitcast.164), calls=%async_computation.4 | async-start | bytes 16777216 | tf_op jit(solution)/shard_map/all_to_all | solution.py:155
  183.6 3.3 pad_maximum_fusion
  186.8 10.0 %gather_fusion.2 = bf16[64,3,2,128,128]{4,3,2,1,0:T(8,128)(2,1)} fusion(bf16[32,3,2,128,128]{4,3,2,0,1:T(8,128)(2,1)} %pad_maximum_fusion, s32[1024]{0:T(1024)S(1)} %pad_clamp_fusion.6), kind=kCustom, calls=%fused_computation.2 | custom fusion | bytes 25166080 | tf_op jit(solution)/shard_map/gather | solution.py:164
  196.8 170.1 %all-to-all-done.4 = bf16[64,2,2,128,128]{4,3,2,1,0:T(8,128)(2,1)} async-done(((bf16[64,2,2,128,128]{4,3,2,1,0:T(8,128)(2,1)}), bf16[64,2,2,128,128]{4,3,2,1,0:T(8,128)(2,1)}, u32[]{:S(2)}, u32[]{:S(2)}) %all-to-all-start.4) | async-done | bytes 8388640 | tf_op jit(solution)/shard_map/all_to_all | solution.py:155
  366.9 6.2 all-to-all-start.2
  377.1 221.7 %all-reduce.2.cloned.1.call-done = bf16[4,2,128,128]{3,2,1,0:T(8,128)(2,1)} async-done(((bf16[4,2,128,128]{3,2,1,0:T(8,128)(2,1)}), bf16[4,2,128,128]{3,2,1,0:T(8,128)(2,1)}) %all-reduce.2.cloned.1.call-update) | async-done | bytes 262160 | tf_op jit(solution)/shard_map/psum | solution.py:25
  602.2 2.3 gather_fusion.1
  605.5 10.0 %gather_fusion.9 = bf16[128,2,128,128]{3,2,1,0:T(8,128)(2,1)} fusion(bf16[128,2,128,128]{3,2,1,0:T(8,128)(2,1)} %bitcast.39, s32[1024]{0:T(1024)S(1)} %pad_clamp_fusion.1), kind=kCustom, calls=%fused_computation.9 | custom fusion | bytes 16777728 | tf_op jit(solution)/shard_map/gather | solution.py:156
  615.5 6.4 gather_fusion.10
  621.9 5.2 multiply_reduce_fusion
  627.5 24.5 %all-to-all-done.2 = bf16[64,1,3,2,128,128]{5,4,3,2,1,0:T(8,128)(2,1)} async-done(((bf16[64,1,3,2,128,128]{5,4,3,2,1,0:T(8,128)(2,1)}), bf16[64,1,3,2,128,128]{5,4,3,2,1,0:T(8,128)(2,1)}, u32[]{:S(2)}, u32[]{:S(2)}) %all-to-all-start.2) | async-done | bytes 12582944 | tf_op jit(solution)/shard_map/all_to_all | solution.py:167
  652.0 8.7 %gather_fusion.3 = bf16[32,3,2,128,128]{4,3,2,1,0:T(8,128)(2,1)} fusion(bf16[64,3,2,128,128]{4,3,2,1,0:T(8,128)(2,1)} %bitcast.28, s32[1024]{0:T(1024)S(1)} %pad_clamp_fusion.5), kind=kCustom, calls=%fused_computation.3 | custom fusion | bytes 12583040 | tf_op jit(solution)/shard_map/gather | solution.py:170
  660.8 5.5 fusion
  666.9 3.3 fusion.18
  670.3 2.7 fusion.20
  674.3 2.1 fusion.1
  676.5 4.1 fusion.12
  680.6 5.5 fusion.31
  (105 shorter events, 26.5 us)
Async XLA Ops:
  6.5 366.9 %copy-start = (s32[4,512]{1,0:T(4,128)S(1)}, s32[4,512]{1,0:T(4,128)}, u32[]{:S(2)}) copy-start(s32[4,512]{1,0:T(4,128)} %param.9) | copy-start | bytes 24580
  10.6 5.7 copy-start.8
  10.6 6.7 copy-start.7
  10.6 52.2 %all-to-all-start = ((bf16[4,1024,512]{1,2,0:T(8,128)(2,1)}), bf16[4,1024,512]{1,2,0:T(8,128)(2,1)}, u32[]{:S(2)}, u32[]{:S(2)}) async-start(bf16[4,1024,512]{1,2,0:T(8,128)(2,1)} %stack.19), calls=%async_computation | async-start | bytes 8388608 | tf_op jit(solution)/shard_map/all_to_all | solution.py:103
  62.8 36.3 %all-to-all-start.3 = ((s32[64,1,2]{2,1,0:T(1,128)}), s32[64,1,2]{2,1,0:T(1,128)S(1)}, u32[]{:S(2)}, u32[]{:S(2)}) async-start(s32[64,1,2]{2,1,0:T(1,128)} %copy.122), calls=%async_computation.3 | async-start | bytes 65536 | tf_op jit(solution)/shard_map/all_to_all | solution.py:153
  99.1 72.7 %all-to-all-start.1 = ((bf16[64,1,128,128]{3,2,1,0:T(8,128)(2,1)}), bf16[64,1,128,128]{3,2,1,0:T(8,128)(2,1)}, u32[]{:S(2)}, u32[]{:S(2)}) async-start(bf16[64,1,128,128]{3,2,1,0:T(8,128)(2,1)} %bitcast.169), calls=%async_computation.1 | async-start | bytes 4194304 | tf_op jit(solution)/shard_map/all_to_all | solution.py:166
  110.6 46.8 %collective-permute-start = (bf16[128,2,4,128]{3,0,2,1:T(8,128)(2,1)}, bf16[128,2,4,128]{3,0,2,1:T(8,128)(2,1)S(1)}, u32[]{:S(2)}, u32[]{:S(2)}) collective-permute-start(bf16[128,2,4,128]{3,0,2,1:T(8,128)(2,1)} %bitcast.160), channel_id=1, source_target_pairs={{0,4},{4,8},{8,12},{12,16},{16,20},{20,24},{24,28},{28,32},{32,36}... | collective-permute-start | bytes 786440 | tf_op jit(solution)/shard_map/ppermute | solution.py:15
  114.8 44.9 %collective-permute-start.1 = (bf16[128,2,4,128]{3,0,2,1:T(8,128)(2,1)}, bf16[128,2,4,128]{3,0,2,1:T(8,128)(2,1)}, u32[]{:S(2)}, u32[]{:S(2)}) collective-permute-start(bf16[128,2,4,128]{3,0,2,1:T(8,128)(2,1)} %bitcast.159), channel_id=1, source_target_pairs={{4,0},{8,4},{12,8},{16,12},{20,16},{24,20},{28,24},{32,28},{36,32}... | collective-permute-start | bytes 786440 | tf_op jit(solution)/shard_map/ppermute | solution.py:18
  161.2 3.8 copy-start.3
  171.8 195.1 %all-to-all-start.4 = ((bf16[64,2,2,128,128]{4,3,2,1,0:T(8,128)(2,1)}), bf16[64,2,2,128,128]{4,3,2,1,0:T(8,128)(2,1)}, u32[]{:S(2)}, u32[]{:S(2)}) async-start(bf16[64,2,2,128,128]{4,3,2,1,0:T(8,128)(2,1)} %bitcast.164), calls=%async_computation.4 | async-start | bytes 16777216 | tf_op jit(solution)/shard_map/all_to_all | solution.py:155
  181.1 2.2 copy-start.5
  366.9 7.9 %copy-start.9 = (s32[32]{0:T(128)S(1)}, s32[32]{0:T(128)}, u32[]{:S(2)}) copy-start(s32[32]{0:T(128)} %get-tuple-element.21) | copy-start | bytes 388
  366.9 285.1 %all-to-all-start.2 = ((bf16[64,1,3,2,128,128]{5,4,3,2,1,0:T(8,128)(2,1)}), bf16[64,1,3,2,128,128]{5,4,3,2,1,0:T(8,128)(2,1)}, u32[]{:S(2)}, u32[]{:S(2)}) async-start(bf16[64,1,3,2,128,128]{5,4,3,2,1,0:T(8,128)(2,1)} %bitcast.163), calls=%async_computation.2 | async-start | bytes 25165824 | tf_op jit(solution)/shard_map/all_to_all | solution.py:167
  373.1 225.7 %all-reduce.2.cloned.1.call-start = ((), (), s32[]{:S(2)}) async-start(), calls=%async_computation.5 | async-start | bytes 524288 | tf_op jit(solution)/shard_map/psum | solution.py:25
  652.0 8.7 %copy-start.6 = (bf16[32,2,128,128]{3,2,0,1:T(8,128)(2,1)S(1)}, bf16[32,2,128,128]{3,2,0,1:T(8,128)(2,1)}, u32[]{:S(2)}) copy-start(bf16[32,2,128,128]{3,2,0,1:T(8,128)(2,1)} %copy.162) | copy-start | bytes 6291460
  666.9 3.4 copy-start.2
  670.3 4.0 copy-start.4
  670.3 10.2 %slice-start = ((s8[6291456]{0:T(1024)(128)(4,1)}), s8[4194304]{0:T(1024)(128)(4,1)S(1)}, s32[]{:S(2)}) async-start(s8[6291456]{0:T(1024)(128)(4,1)} %bitcast.173), calls=%async_computation.6 | async-start | bytes 8388608
  674.3 6.2 slice-start.1
  680.6 5.5 copy-start.1
Sparse Core Ops, SparseCore 0:
  377.4 221.3 all-reduce.1
